TPU v7x, 512 devices: a whole 4x8x8 slice. The times are simulated.
512 devices in a mesh: expert: 32 (over x, z_hi, core), tensor: 8 (over y), dp: 2 (over z_lo).
Axes of the slice: x: 4, y: 8, z: 8 (z_hi: 4, z_lo: 2; z = z_hi * 2 + z_lo), core: 2. Of those that a mesh axis runs over, the one named last changes fastest.
Arguments:
- tokens: bfloat16 [6144, 5120], P(('dp', 'expert'), 'tensor'), parts along dimension 0, may hold values from -6 to 6
- routes: int32 [6144, 6], P(('dp', 'expert')), parts along dimension 0, may hold values from 0 to 31, all different within a row; in each aligned block of 96 rows (0 to 95, 96 to 191, ...) at most 18 rows name the same one
- gates: float32 [6144, 6], P(('dp', 'expert')), parts along dimension 0, may hold values from 0.05 to 0.6
- gate_up: bfloat16 [32, 5120, 2, 1024], P('expert', None, None, 'tensor'), may hold values from -0.078125 to 0.078125
- down_weight: bfloat16 [32, 5120, 1024], P('expert', None, 'tensor'), may hold values from -0.1875 to 0.1875
- old_map: int32 [32], replicated, may hold values from 0 to 31, each once
- new_map: int32 [32], replicated, may hold values from 0 to 31, each once
Outputs:
- mixed: bfloat16 [6144, 5120], P(('dp', 'expert'), 'tensor'), parts along dimension 0
There are 2 independent parts, one for each index of `dp`. A program takes and returns all parts, laid end to end along the dimension named above; an argument that names none is the same for every part. Nothing has to cross between parts.
Inputs may be any that keep to these rules, and one draw needn't show every extreme that they name: `routes`: each row names 6 different slots; in each aligned block of 96 rows (the rows of one index of expert) no slot is named by more than 18 rows; since each row names 6 different slots, every slot is then named by exactly 18 rows of every block. `old_map`: each expert appears exactly once. `new_map`: each expert appears exactly once.
All inputs are finite; a program needn't handle non-finite values.
Results may differ from a plain program's by a relative error of at most 0.0058.
Values may be sent and summed in bfloat16 or wider, within the bound.
No kernel may reach another device: no remote copies, remote signals or barrier semaphores. Data moves between devices by JAX's collectives and lax.ppermute only.
A program may use at most 64 MiB of HBM per device.

v0:
```python
import jax
import jax.numpy as jnp
from jax import lax
from jax.sharding import Mesh
from jax.sharding import PartitionSpec as P

EXPERT = ("expert_0", "expert_1", "expert_2")
DP_EXPERT = ("dp", "expert_0", "expert_1", "expert_2")


def in_blocks(x, dim, size):
    lengths = x.shape
    parts = x.reshape(*lengths[:dim], size, lengths[dim] // size, *lengths[dim + 1 :])
    return jnp.moveaxis(parts, dim, 0)


def laid_out(parts, dim):
    parts = jnp.moveaxis(parts, 0, dim)
    lengths = parts.shape
    return parts.reshape(*lengths[:dim], lengths[dim] * lengths[dim + 1], *lengths[dim + 2 :])


def exchange_in_order(parts, axes, order):
    lengths = [lax.axis_size(a) for a in axes]
    parts = parts.reshape(*lengths, *parts.shape[1:])
    for k in order:
        parts = lax.all_to_all(parts, axes[k], split_axis=k, concat_axis=k, tiled=True)
    return parts.reshape(-1, *parts.shape[len(axes) :])


def core_and_chips(x, groups, order, split_dim, concat_dim):
    size = lax.axis_size(groups[0]) * lax.axis_size(groups[1])
    parts = in_blocks(x, split_dim, size)
    return laid_out(exchange_in_order(parts, groups, order), concat_dim)


def from_everyone(x, axis):
    size = lax.axis_size(axis)
    return lax.all_to_all(jnp.broadcast_to(x[None], (size, *x.shape)), axis, 0, 0, tiled=True)


def collect(x, axis, dim):
    parts = from_everyone(x, axis)
    return laid_out(parts, dim)


def local(tokens, routes, gates, gate_up, down_weight, old_map, new_map):
    experts = lax.axis_size(EXPERT)
    tensor_count = lax.axis_size("tensor")
    tok_rows = tokens.shape[0]
    feature_part = tokens.shape[1]
    picks_row = routes.shape[1]
    capacity = (tok_rows * picks_row + experts - 1) // experts
    width = gate_up.shape[1]
    hidden = down_weight.shape[2]
    buffer_rows = experts * capacity
    slot_ids = jnp.arange(experts, dtype=jnp.int32)
    holder = jnp.sum(jnp.where(new_map[:, None] == old_map[None, :], slot_ids[None, :], 0), axis=1)
    weight_in = gate_up.reshape(width, 2 * hidden)
    weight_out = down_weight.reshape(width, hidden)
    target = jnp.sum(
        jnp.where(routes[:, :, None] == slot_ids[None, None, :], holder[None, None, :], 0), axis=2
    )
    flat_target = target.reshape(-1)
    onehot = (flat_target[:, None] == slot_ids[None, :]).astype(jnp.int32)
    earlier = jnp.cumsum(onehot, axis=0) - onehot
    position = jnp.sum(earlier * onehot, axis=1)
    slot_index = flat_target * capacity + position
    columns = jnp.arange(buffer_rows, dtype=jnp.int32)
    matches = (slot_index[:, None] == columns[None, :]).reshape(tok_rows, picks_row, buffer_rows)
    assign = jnp.sum(matches.astype(jnp.float32), axis=1).astype(jnp.bfloat16)
    combine_weights = jnp.sum(jnp.where(matches, gates[:, :, None], 0.0), axis=1)
    outgoing = lax.dot_general(
        assign, tokens, (((0,), (0,)), ((), ())), preferred_element_type=jnp.float32
    )
    outgoing = outgoing.astype(jnp.bfloat16).reshape(experts, capacity, feature_part)
    arrived = core_and_chips(outgoing, (("expert_0", "expert_1"), "expert_2"), (1, 0), 0, 0)
    piece = lax.all_gather(arrived, "tensor", axis=2, tiled=True)
    flat_piece = piece.reshape(buffer_rows, piece.shape[2])
    projected = jnp.dot(flat_piece, weight_in, preferred_element_type=jnp.float32)
    activation = (jax.nn.silu(projected[:, :hidden]) * projected[:, hidden:]).astype(jnp.bfloat16)
    down_parts = weight_out.reshape(tensor_count, width // tensor_count, hidden)
    down_mine = lax.all_to_all(
        down_parts, "tensor", split_axis=0, concat_axis=2, tiled=True
    ).reshape(width // tensor_count, tensor_count * hidden)
    summed = lax.dot_general(
        collect(activation, "tensor", 1),
        down_mine,
        (((1,), (1,)), ((), ())),
        preferred_element_type=jnp.float32,
    )
    expert_out = summed.astype(jnp.bfloat16).reshape(experts, capacity, feature_part)
    returned = lax.all_to_all(expert_out, EXPERT, split_axis=0, concat_axis=0, tiled=True)
    gathered_back = returned.reshape(buffer_rows, feature_part).astype(jnp.float32)
    mixed = jnp.dot(
        combine_weights,
        gathered_back,
        precision=lax.Precision.HIGHEST,
        preferred_element_type=jnp.float32,
    )
    return mixed.astype(jnp.bfloat16)


def solution(mesh):
    split = Mesh(
        mesh.devices.reshape(4, 4, 2, mesh.shape["tensor"], mesh.shape["dp"]),
        ("expert_0", "expert_1", "expert_2", "tensor", "dp"),
    )
    in_specs = (
        P(DP_EXPERT, "tensor"),
        P(DP_EXPERT, None),
        P(DP_EXPERT, None),
        P(EXPERT, None, None, "tensor"),
        P(EXPERT, None, "tensor"),
        P(),
        P(),
    )
    out_specs = P(DP_EXPERT, "tensor")
    return jax.shard_map(local, mesh=split, in_specs=in_specs, out_specs=out_specs, check_vma=False)
```

profile of v0, /device:TPU:64, one launch (start us, length us, event | category | flops | bytes accessed | tf_op | source)
XLA Modules:
  0.0 253.1 jit_solution(2696037991912060983)
XLA Ops:
  6.5 0.0 copy-start
  6.5 0.0 all-gather.2.cloned.1.call-start
  6.5 0.9 select_reduce_fusion.2
  7.4 0.8 select_reduce_fusion.1
  8.2 0.1 copy.37
  8.3 0.1 eq.68
  8.5 1.5 reduce-window.6
  10.0 0.3 slice_reduce_fusion
  10.2 0.1 bitcast_bitcast_fusion
  10.4 0.1 reduce_sum.50
  10.5 0.1 copy.40
  10.6 1.1 convert_reduce_fusion
  11.7 0.0 copy-done
  11.7 0.4 convolution_convert_fusion.1
  12.1 0.2 reshape_reshape_reshape.3
  12.3 0.1 copy.41
  12.4 4.3 %all_to_all.35 = bf16[16,2,1,18,640]{4,0,3,2,1:T(8,128)(2,1)S(1)} all-to-all(bf16[16,2,1,18,640]{4,0,3,2,1:T(8,128)(2,1)S(1)} %copy.41), channel_id=1, replica_groups=mesh['expert_0'=4,'expert_1'=4,'expert_2'=2,'tensor'=8,'dp'=2] {'expert_2'}, dimensions={1} | all-to-all | bytes 1474560 | tf_op jit(solution)/shard_map/all_to_all | solution.py:27
  16.7 0.6 copy.42
  17.3 35.1 %all_to_all.36 = bf16[16,2,1,18,640]{4,1,3,2,0:T(2,128)(2,1)S(1)} all-to-all(bf16[16,2,1,18,640]{4,1,3,2,0:T(2,128)(2,1)S(1)} %copy.42), channel_id=1, replica_groups=mesh['expert_0'=4,'expert_1'=4,'expert_2'=2,'tensor'=8,'dp'=2] {'expert_..., dimensions={0} | all-to-all | bytes 1474560 | tf_op jit(solution)/shard_map/all_to_all | solution.py:27
  52.4 0.5 copy.43
  52.9 1.1 reshape_reshape.6
  54.0 0.0 all-gather.2.cloned.1.call-update
  54.1 7.1 %all-to-all-start.3 = ((bf16[8,640,128]{2,1,0:T(8,128)(2,1)}), bf16[8,640,128]{2,1,0:T(8,128)(2,1)S(1)}, u32[]{:S(2)}, u32[]{:S(2)}) async-start(bf16[8,640,128]{2,1,0:T(8,128)(2,1)} %bitcast.2), calls=%async_computation.3 | async-start | bytes 2621440 | tf_op jit(solution)/shard_map/all_to_all | solution.py:83
  61.2 86.8 %all-gather.2.cloned.1.call-done = bf16[32,18,5120]{2,0,1:T(8,128)(2,1)} async-done(((bf16[32,18,640]{2,0,1:T(8,128)(2,1)}), bf16[32,18,5120]{2,0,1:T(8,128)(2,1)}) %all-gather.2.cloned.1.call-update) | async-done | bytes 5898256 | tf_op jit(solution)/shard_map/all_gather | solution.py:78
  148.0 9.2 %copy.44 = bf16[32,18,5120]{2,1,0:T(8,128)(2,1)} copy(bf16[32,18,5120]{2,0,1:T(8,128)(2,1)} %all-gather.2.cloned.1.call-done) | data formatting | bytes 11796480 | tf_op jit(solution)/shard_map/all_gather | solution.py:78
  157.1 8.8 %reshape.57 = bf16[576,5120]{1,0:T(8,128)(2,1)} reshape(bf16[32,18,5120]{2,1,0:T(8,128)(2,1)} %copy.44) | data formatting | bytes 11796480 | tf_op jit(solution)/shard_map/reshape | solution.py:79
  165.9 5.2 %fusion = f32[576,256]{1,0:T(8,128)S(1)} fusion(bf16[576,5120]{1,0:T(8,128)(2,1)} %reshape.57, bf16[640,8,2,128]{3,2,1,0:T(2,128)(2,1)} %bitcast.42), kind=kOutput, calls=%fused_computation | convolution fusion | flops 1509949440 | bytes 9109504 | tf_op jit(solution)/shard_map/dot_general | solution.py:80
  171.1 0.1 fusion.5
  171.2 0.0 all-to-all-done.3
  171.2 1.2 broadcast_in_dim.58
  172.4 4.5 %all-to-all-start.2 = ((bf16[8,576,128]{2,1,0:T(8,128)(2,1)}), bf16[8,576,128]{2,1,0:T(8,128)(2,1)}, u32[]{:S(2)}, u32[]{:S(2)}) async-start(bf16[8,576,128]{2,1,0:T(8,128)(2,1)} %broadcast_in_dim.58), calls=%async_computation.2 | async-start | bytes 2359296 | tf_op jit(solution)/shard_map/all_to_all | solution.py:39
  176.9 0.7 copy.46
  177.6 31.1 %all-to-all-done.2 = bf16[8,576,128]{2,1,0:T(8,128)(2,1)} async-done(((bf16[8,576,128]{2,1,0:T(8,128)(2,1)}), bf16[8,576,128]{2,1,0:T(8,128)(2,1)}, u32[]{:S(2)}, u32[]{:S(2)}) %all-to-all-start.2) | async-done | bytes 1179680 | tf_op jit(solution)/shard_map/all_to_all | solution.py:39
  208.8 3.3 %convolution_convert_fusion = bf16[576,640]{1,0:T(8,128)(2,1)} fusion(bf16[640,1024]{0,1:T(8,128)(2,1)S(1)} %bitcast.40, bf16[8,576,128]{2,1,0:T(8,128)(2,1)} %all-to-all-done.2), kind=kOutput, calls=%fused_computation.6 | convolution fusion | flops 755343360 | bytes 3227648 | tf_op jit(solution)/shard_map/dot_general | solution.py:86
  212.0 1.3 reshape.61
  213.3 31.5 %all_to_all.37 = bf16[32,18,640]{2,1,0:T(8,128)(2,1)S(1)} all-to-all(bf16[32,18,640]{2,1,0:T(8,128)(2,1)S(1)} %reshape.61), channel_id=1, replica_groups=mesh['expert_0'=4,'expert_1'=4,'expert_2'=2,'tensor'=8,'dp'=2] {'expert_..., dimensions={0} | all-to-all | bytes 1474560 | tf_op jit(solution)/shard_map/all_to_all | solution.py:93
  244.8 0.2 reshape.62
  245.0 1.2 convolution_convert_fusion.2
  (5 shorter events, 0.1 us)
Async XLA Ops:
  6.5 5.1 %copy-start = (bf16[96,640]{1,0:T(8,128)(2,1)S(1)}, bf16[96,640]{1,0:T(8,128)(2,1)}, u32[]{:S(2)}) copy-start(bf16[96,640]{1,0:T(8,128)(2,1)} %param.7) | copy-start | bytes 368644
  6.5 141.4 %all-gather.2.cloned.1.call-start = ((), (), s32[]{:S(2)}) async-start(), calls=%async_computation.5 | async-start | bytes 6635520 | tf_op jit(solution)/shard_map/all_gather | solution.py:78
  54.1 117.1 %all-to-all-start.3 = ((bf16[8,640,128]{2,1,0:T(8,128)(2,1)}), bf16[8,640,128]{2,1,0:T(8,128)(2,1)S(1)}, u32[]{:S(2)}, u32[]{:S(2)}) async-start(bf16[8,640,128]{2,1,0:T(8,128)(2,1)} %bitcast.2), calls=%async_computation.3 | async-start | bytes 2621440 | tf_op jit(solution)/shard_map/all_to_all | solution.py:83
  172.4 36.4 %all-to-all-start.2 = ((bf16[8,576,128]{2,1,0:T(8,128)(2,1)}), bf16[8,576,128]{2,1,0:T(8,128)(2,1)}, u32[]{:S(2)}, u32[]{:S(2)}) async-start(bf16[8,576,128]{2,1,0:T(8,128)(2,1)} %broadcast_in_dim.58), calls=%async_computation.2 | async-start | bytes 2359296 | tf_op jit(solution)/shard_map/all_to_all | solution.py:39
Sparse Core Ops, SparseCore 0:
  54.2 93.7 all-gather.1
where the time goes:
time: 254 us; the launch traced here: 253 us
  waiting for transfers between devices  118 us (46%)
  blocking collectives  70.8 us (28%)
  local copies, waits for them, and re-layouts  24.6 us (10%)
  between operations  13.5 us (5%)
  starting transfers between devices  11.7 us (5%)
  matrix products  10 us (4%)
  other arithmetic  4.47 us (2%)
    all_gather x1, waiting for transfers between devices, local(): piece = lax.all_gather(arrived, 'tensor', axis=2, tiled=True)  86.8 us
    all_to_all x2, blocking collectives, exchange_in_order(): lax.all_to_all(parts, axes[k], split_axis=k, concat_axis=k, tiled=True)  39.4 us
    all_to_all x1, blocking collectives, local(): lax.all_to_all(expert_out, EXPERT, split_axis=0, concat_axis=0, tiled=True)  31.5 us
    all_to_all x1, waiting for transfers between devices, from_everyone(): lax.all_to_all(jnp.broadcast_to(x[None], (size, *x.shape)), axis, 0, 0, t...  31.1 us
    all_gather x1, local copies, waits for them, and re-layouts, local(): piece = lax.all_gather(arrived, 'tensor', axis=2, tiled=True)  9.16 us
    reshape x1, local copies, waits for them, and re-layouts, local(): flat_piece = piece.reshape(buffer_rows, piece.shape[2])  8.78 us
    all_to_all x1, starting transfers between devices, local(): lax.all_to_all(down_parts, 'tensor', split_axis=0, concat_axis=2, tiled=T...  7.11 us
    dot_general x1, matrix products, local(): jnp.dot(flat_piece, weight_in, preferred_element_type=jnp.float32)  5.15 us
  transfers between devices with their start and end apart: 3, of which 2 were waited for; matrix products, arithmetic and copies ran while one was open for 9% of the time, Pallas kernels for 0%

commit v1 on v0

--- a/solution.py
+++ b/solution.py
@@ -75,7 +75,8 @@
     )
     outgoing = outgoing.astype(jnp.bfloat16).reshape(experts, capacity, feature_part)
     arrived = core_and_chips(outgoing, (("expert_0", "expert_1"), "expert_2"), (1, 0), 0, 0)
-    piece = lax.all_gather(arrived, "tensor", axis=2, tiled=True)
+    sent = jnp.stack([arrived] * lax.axis_size("tensor"))
+    piece = jnp.concatenate(lax.all_to_all(sent, "tensor", 0, 0), axis=2)
     flat_piece = piece.reshape(buffer_rows, piece.shape[2])
     projected = jnp.dot(flat_piece, weight_in, preferred_element_type=jnp.float32)
     activation = (jax.nn.silu(projected[:, :hidden]) * projected[:, hidden:]).astype(jnp.bfloat16)

time: 254 us -> 298 us (1.17)
  blocking collectives: 70.8 us -> 211 us
  waiting for transfers between devices: 118 us -> 53.6 us
  between operations: 13.5 us -> 0.19 us
  local copies, waits for them, and re-layouts: 24.6 us -> 14.2 us
  starting transfers between devices: 11.7 us -> 8 us
  matrix products: 10 us -> 6.54 us
    all_to_all x0 -> x1, blocking collectives: none -> 139 us  [local(): piece = jnp.concatenate(lax.all_to_all(sent, 'tensor', 0, 0), axis=2)]
    all_gather x1 -> x0, waiting for transfers between devices: 86.8 us -> none  [local(): piece = lax.all_gather(arrived, 'tensor', axis=2, tiled=True)]
    all_to_all x1, waiting for transfers between devices: 0.01 us -> 22.6 us  [local(): lax.all_to_all(down_parts, 'tensor', split_axis=0, concat_axis=2, tiled=T...]
    all_gather x1 -> x0, local copies, waits for them, and re-layouts: 9.16 us -> none  [local(): piece = lax.all_gather(arrived, 'tensor', axis=2, tiled=True)]
    all_to_all x1, starting transfers between devices: 7.11 us -> 3.57 us  [local(): lax.all_to_all(down_parts, 'tensor', split_axis=0, concat_axis=2, tiled=T...]
    dot_general x1, matrix products: 5.15 us -> 1.68 us  [local(): jnp.dot(flat_piece, weight_in, preferred_element_type=jnp.float32)]
  transfers between devices with their start and end apart: 3 -> 2, of which waited for: 2 -> 2; matrix products, arithmetic and copies ran while one was open for 9% -> 3% of each run, Pallas kernels for 0% -> 0%
where the time goes in v1:
time: 298 us
  blocking collectives  211 us (71%)
  waiting for transfers between devices  53.6 us (18%)
  local copies, waits for them, and re-layouts  14.2 us (5%)
  starting transfers between devices  8 us (3%)
  matrix products  6.54 us (2%)
  other arithmetic  4.47 us (2%)
    all_to_all x1, blocking collectives, local(): piece = jnp.concatenate(lax.all_to_all(sent, 'tensor', 0, 0), axis=2)  139 us
    all_to_all x2, blocking collectives, exchange_in_order(): lax.all_to_all(parts, axes[k], split_axis=k, concat_axis=k, tiled=True)  39.4 us
    all_to_all x1, blocking collectives, local(): lax.all_to_all(expert_out, EXPERT, split_axis=0, concat_axis=0, tiled=True)  32.4 us
    all_to_all x1, waiting for transfers between devices, from_everyone(): lax.all_to_all(jnp.broadcast_to(x[None], (size, *x.shape)), axis, 0, 0, t...  31 us
    all_to_all x1, waiting for transfers between devices, local(): lax.all_to_all(down_parts, 'tensor', split_axis=0, concat_axis=2, tiled=T...  22.6 us
    reshape x1, local copies, waits for them, and re-layouts, local(): piece = jnp.concatenate(lax.all_to_all(sent, 'tensor', 0, 0), axis=2)  6.08 us
  transfers between devices with their start and end apart: 2, of which 2 were waited for; matrix products, arithmetic and copies ran while one was open for 3% of the time, Pallas kernels for 0%

profile of v1, /device:TPU:64, one launch (start us, length us, event | category | flops | bytes accessed | tf_op | source)
XLA Modules:
  0.0 297.8 jit_solution(5482845722754498569)
XLA Ops:
  0.0 0.0 copy-start
  0.0 0.9 select_reduce_fusion.2
  0.9 0.8 select_reduce_fusion.1
  1.7 0.1 copy.49
  1.8 0.1 eq.68
  2.0 1.5 reduce-window.6
  3.4 0.3 slice_reduce_fusion
  3.7 0.1 bitcast_bitcast_fusion
  3.8 0.1 reduce_sum.50
  4.0 0.1 copy.52
  4.0 1.1 convert_reduce_fusion
  5.1 0.0 copy-done
  5.1 0.4 convolution_convert_fusion.1
  5.5 0.2 reshape_reshape_reshape.3
  5.8 0.1 copy.53
  5.9 4.3 %all_to_all.40 = bf16[16,2,1,18,640]{4,0,3,2,1:T(8,128)(2,1)S(1)} all-to-all(bf16[16,2,1,18,640]{4,0,3,2,1:T(8,128)(2,1)S(1)} %copy.53), channel_id=1, replica_groups=mesh['expert_0'=4,'expert_1'=4,'expert_2'=2,'tensor'=8,'dp'=2] {'expert_2'}, dimensions={1} | all-to-all | bytes 1474560 | tf_op jit(solution)/shard_map/all_to_all | solution.py:27
  10.2 0.6 copy.54
  10.8 35.1 %all_to_all.41 = bf16[16,2,1,18,640]{4,1,3,2,0:T(2,128)(2,1)S(1)} all-to-all(bf16[16,2,1,18,640]{4,1,3,2,0:T(2,128)(2,1)S(1)} %copy.54), channel_id=1, replica_groups=mesh['expert_0'=4,'expert_1'=4,'expert_2'=2,'tensor'=8,'dp'=2] {'expert_..., dimensions={0} | all-to-all | bytes 1474560 | tf_op jit(solution)/shard_map/all_to_all | solution.py:27
  45.8 0.5 copy.55
  46.3 0.3 stack_reshape_reshape.2
  46.6 0.6 stack.3
  47.3 138.9 %all_to_all.42 = bf16[8,32,18,640]{3,1,2,0:T(8,128)(2,1)} all-to-all(bf16[8,32,18,640]{3,1,2,0:T(8,128)(2,1)S(1)} %stack.3), channel_id=1, replica_groups=mesh['expert_0'=4,'expert_1'=4,'expert_2'=2,'tensor'=8,'dp'=2] {'tensor'}, dimensions={0} | all-to-all | bytes 11796480 | tf_op jit(solution)/shard_map/all_to_all | solution.py:79
  186.2 3.6 %all-to-all-start.4 = ((bf16[8,640,128]{2,1,0:T(8,128)(2,1)}), bf16[8,640,128]{2,1,0:T(8,128)(2,1)S(1)}, u32[]{:S(2)}, u32[]{:S(2)}) async-start(bf16[8,640,128]{2,1,0:T(8,128)(2,1)} %bitcast.3), calls=%async_computation.4 | async-start | bytes 2621440 | tf_op jit(solution)/shard_map/all_to_all | solution.py:84
  189.8 6.1 %copy.56 = bf16[32,18,8,640]{3,2,1,0:T(8,128)(2,1)S(1)} copy(bf16[32,18,8,640]{3,0,1,2:T(8,128)(2,1)} %bitcast.43) | data formatting | bytes 11796480 | tf_op jit(solution)/shard_map/reshape | solution.py:79
  195.8 0.0 copy-start.1
  195.8 1.4 copy.62
  197.2 0.4 copy-done.1
  197.6 1.7 fusion
  199.3 0.1 fusion.5
  199.4 22.6 %all-to-all-done.4 = bf16[8,640,128]{2,1,0:T(8,128)(2,1)S(1)} async-done(((bf16[8,640,128]{2,1,0:T(8,128)(2,1)}), bf16[8,640,128]{2,1,0:T(8,128)(2,1)S(1)}, u32[]{:S(2)}, u32[]{:S(2)}) %all-to-all-start.4) | async-done | bytes 1310752 | tf_op jit(solution)/shard_map/all_to_all | solution.py:84
  221.9 1.2 broadcast_in_dim.58
  223.1 4.4 %all-to-all-start.3 = ((bf16[8,576,128]{2,1,0:T(8,128)(2,1)}), bf16[8,576,128]{2,1,0:T(8,128)(2,1)}, u32[]{:S(2)}, u32[]{:S(2)}) async-start(bf16[8,576,128]{2,1,0:T(8,128)(2,1)} %broadcast_in_dim.58), calls=%async_computation.3 | async-start | bytes 2359296 | tf_op jit(solution)/shard_map/all_to_all | solution.py:39
  227.6 0.7 copy.58
  228.3 31.0 %all-to-all-done.3 = bf16[8,576,128]{2,1,0:T(8,128)(2,1)} async-done(((bf16[8,576,128]{2,1,0:T(8,128)(2,1)}), bf16[8,576,128]{2,1,0:T(8,128)(2,1)}, u32[]{:S(2)}, u32[]{:S(2)}) %all-to-all-start.3) | async-done | bytes 1179680 | tf_op jit(solution)/shard_map/all_to_all | solution.py:39
  259.3 3.3 %convolution_convert_fusion = bf16[576,640]{1,0:T(8,128)(2,1)} fusion(bf16[640,1024]{0,1:T(8,128)(2,1)S(1)} %bitcast.47, bf16[8,576,128]{2,1,0:T(8,128)(2,1)} %all-to-all-done.3), kind=kOutput, calls=%fused_computation.6 | convolution fusion | flops 755343360 | bytes 3227648 | tf_op jit(solution)/shard_map/dot_general | solution.py:87
  262.6 1.3 reshape.63
  263.9 32.4 %all_to_all.43 = bf16[32,18,640]{2,1,0:T(8,128)(2,1)S(1)} all-to-all(bf16[32,18,640]{2,1,0:T(8,128)(2,1)S(1)} %reshape.63), channel_id=1, replica_groups=mesh['expert_0'=4,'expert_1'=4,'expert_2'=2,'tensor'=8,'dp'=2] {'expert_..., dimensions={0} | all-to-all | bytes 1474560 | tf_op jit(solution)/shard_map/all_to_all | solution.py:94
  296.3 0.2 reshape.64
  296.6 1.2 convolution_convert_fusion.2
  (5 shorter events, 0.1 us)
Async XLA Ops:
  0.0 5.1 %copy-start = (bf16[96,640]{1,0:T(8,128)(2,1)S(1)}, bf16[96,640]{1,0:T(8,128)(2,1)}, u32[]{:S(2)}) copy-start(bf16[96,640]{1,0:T(8,128)(2,1)} %param.7) | copy-start | bytes 368644
  186.2 35.8 %all-to-all-start.4 = ((bf16[8,640,128]{2,1,0:T(8,128)(2,1)}), bf16[8,640,128]{2,1,0:T(8,128)(2,1)S(1)}, u32[]{:S(2)}, u32[]{:S(2)}) async-start(bf16[8,640,128]{2,1,0:T(8,128)(2,1)} %bitcast.3), calls=%async_computation.4 | async-start | bytes 2621440 | tf_op jit(solution)/shard_map/all_to_all | solution.py:84
  195.8 1.7 copy-start.1
  223.1 36.2 %all-to-all-start.3 = ((bf16[8,576,128]{2,1,0:T(8,128)(2,1)}), bf16[8,576,128]{2,1,0:T(8,128)(2,1)}, u32[]{:S(2)}, u32[]{:S(2)}) async-start(bf16[8,576,128]{2,1,0:T(8,128)(2,1)} %broadcast_in_dim.58), calls=%async_computation.3 | async-start | bytes 2359296 | tf_op jit(solution)/shard_map/all_to_all | solution.py:39
